TPU v7x, 32 devices: a whole 2x2x4 slice. The times are simulated.
32 devices in a mesh: tm: 4 (over y, x), op: 8 (over z, core).
Axes of the slice: x: 2, y: 2, z: 4, core: 2. Of those that a mesh axis runs over, the one named last changes fastest.
Arguments:
- sink_elem: bfloat16 [2, 4, 2048, 16384], P(None, 'tm', 'op'), may hold values from -6 to 6
- source_elem: bfloat16 [2, 2, 2048, 16384], P(None, None, None, 'op'), may hold values from -6 to 6
- peram: bfloat16 [2, 4, 2, 512, 512], P(None, 'tm', None, 'op'), may hold values from -4 to 4
- pair_list: int32 [16, 1], replicated, may hold values from 0 to 15
- spin_sets: int32 [16, 3], replicated, may hold values from 0 to 3
Outputs:
- correlator: float32 [2, 4, 2, 16, 1], P(None, 'tm')
All inputs are finite; a program needn't handle non-finite values.
Results may differ from a plain program's by a relative error of at most 0.0041.
Values may be sent and summed in bfloat16 or wider, within the bound.
No kernel may reach another device: no remote copies, remote signals or barrier semaphores. Data moves between devices by JAX's collectives and lax.ppermute only.
A program may use at most 256 MiB of HBM per device.

v0:
```python
import jax
import jax.numpy as jnp
from jax import lax
from jax.sharding import PartitionSpec as P

NEV = 128
NSPIN = 4
NOP = 16
TSRC = 2
PAIRS = 1


def complex_matrix(block):
    upper = jnp.concatenate([block[0], block[1]], axis=1)
    lower = jnp.concatenate([-block[1], block[0]], axis=1)
    return jnp.stack([upper, lower])


def on_device(sink_elem, source_elem, peram, pair_list, spin_sets):
    tau_all = lax.all_gather(peram, "op", axis=3, tiled=True)
    position = lax.axis_index("op")
    rows = sink_elem.shape[2]
    local_times = sink_elem.shape[1]
    span = min(rows, NEV)
    groups = rows // span
    cols = source_elem.shape[3]

    def spin_block(local, t0, left, right):
        return lax.dynamic_slice(tau_all[:, local, t0], (0, left * NEV, right * NEV), (2, NEV, NEV))

    def sink_side(local, t0, p):
        pieces = []
        for group in range(groups):
            op_now = (position * rows + group * span) // NEV
            mine = spin_sets[op_now]
            theirs = spin_sets[pair_list[op_now, p]]
            third = complex_matrix(spin_block(local, t0, mine[2], theirs[2]))
            second = complex_matrix(spin_block(local, t0, mine[1], theirs[1]))
            phi = sink_elem[:, local, group * span : (group + 1) * span].reshape(2, span * NEV, NEV)
            x_both = jnp.einsum("cxk,ckb->xb", phi, third, preferred_element_type=jnp.float32)
            x_both = x_both.astype(jnp.bfloat16).reshape(span, NEV, 2, NEV)
            y_both = jnp.einsum("ijck,cjb->ibk", x_both, second, preferred_element_type=jnp.float32)
            y_both = y_both.astype(jnp.bfloat16).reshape(span, 2, NEV * NEV)
            pieces.append(jnp.transpose(y_both, (1, 0, 2)))
        return jnp.concatenate(pieces, axis=1)

    partial_terms = {}
    for t0 in range(TSRC):
        combos = [(local, t0, p) for local in range(local_times) for p in range(PAIRS)]
        stacked = jnp.stack([sink_side(local, t0, p) for local, t0, p in combos], axis=1)
        columns = lax.all_to_all(stacked, "op", split_axis=3, concat_axis=2, tiled=True)
        for index, combo in enumerate(combos):
            column_t0 = combo[1]
            other = pair_list[:, combo[2]]
            source = source_elem[:, column_t0].reshape(2, NOP, NEV, cols)
            chosen = jnp.take(source, other, axis=1)
            tiles = columns[:, index].reshape(2, NOP, NEV, cols)

            def inner(a, b):
                return jnp.einsum("oic,ojc->oij", a, b, preferred_element_type=jnp.float32)

            m_re = inner(tiles[0], chosen[0]) + inner(tiles[1], chosen[1])
            m_im = inner(tiles[1], chosen[0]) - inner(tiles[0], chosen[1])
            blocks = tau_all[:, combo[0], column_t0].reshape(2, NSPIN, NEV, NSPIN, NEV)
            blocks = jnp.transpose(blocks, (1, 3, 0, 2, 4))
            first = blocks[spin_sets[:, 0], spin_sets[other, 0]].astype(jnp.float32)
            c_re = jnp.sum(first[:, 0] * m_re - first[:, 1] * m_im, axis=(1, 2))
            c_im = jnp.sum(first[:, 0] * m_im + first[:, 1] * m_re, axis=(1, 2))
            partial_terms[combo] = jnp.stack([c_re, c_im])
    local = 0
    per_time = []
    for t0 in range(TSRC):
        per_time.append(jnp.stack([partial_terms[local, t0, 0]], axis=-1))
    per_local = [jnp.stack(per_time, axis=1)]
    partial_sum = jnp.stack(per_local, axis=1)
    totals = lax.psum(partial_sum, "op")
    return totals * (1.0 / float(NEV**3))


def solution(mesh):
    in_specs = (
        P(None, "tm", "op", None),
        P(None, None, None, "op"),
        P(None, "tm", None, "op", None),
        P(),
        P(),
    )
    out_specs = P(None, "tm", None, None, None)
    return jax.shard_map(
        on_device, mesh=mesh, in_specs=in_specs, out_specs=out_specs, check_vma=False
    )
```

profile of v0, /device:TPU:0, one launch (start us, length us, event | category | flops | bytes accessed | tf_op | source)
XLA Modules:
  0.0 1121.4 jit_solution(15769526317778974320)
XLA Ops:
  20.9 11.6 %fusion.86 = (bf16[2,1,128,16384]{3,2,1,0:T(8,128)(2,1)}, bf16[2,1,128,16384]{3,2,1,0:T(8,128)(2,1)}) fusion(bf16[2,1,256,16384]{3,2,1,0:T(8,128)(2,1)} %param.7), kind=kLoop, calls=%fused_computation.166 | loop fusion | bytes 33554432 | tf_op jit(solution)/shard_map/slice | solution.py:39
  32.5 13.5 %reshape_squeeze.23 = bf16[2,16384,128]{2,1,0:T(8,128)(2,1)} reshape(bf16[2,1,128,16384]{3,2,1,0:T(8,128)(2,1)} %get-tuple-element.32) | data formatting | bytes 16777216 | tf_op jit(solution)/shard_map/reshape;squeeze | solution.py:39
  45.9 13.5 %reshape_squeeze.24 = bf16[2,16384,128]{2,1,0:T(8,128)(2,1)} reshape(bf16[2,1,128,16384]{3,2,1,0:T(8,128)(2,1)} %get-tuple-element.33) | data formatting | bytes 16777216 | tf_op jit(solution)/shard_map/reshape;squeeze | solution.py:39
  89.1 26.0 %fusion.18 = bf16[128,256,128]{2,1,0:T(8,128)(2,1)} fusion(bf16[128,128,2,128]{1,0,3,2:T(8,128)(2,1)} %bitcast.312, bf16[1,128,256]{1,2,0:T(8,128)(2,1)S(1)} %get-tuple-element.57, bf16[1,128,256]{1,2,0:T(8,128)(2,1)S(1)} %get-tuple-element.56), kind=kOutput, calls=%fused_computation.43 | convolution fusion | flops 2151940096 | bytes 16908288 | tf_op jit(solution)/shard_map/ijck,cjb->ibk/dot_general | solution.py:42
  115.1 12.7 %reshape.125 = bf16[128,2,16384]{2,1,0:T(2,128)(2,1)} reshape(bf16[128,256,128]{2,1,0:T(8,128)(2,1)} %fusion.18) | data formatting | bytes 16777216 | tf_op jit(solution)/shard_map/reshape | solution.py:43
  127.8 12.0 %copy.116 = bf16[128,2,16384]{2,0,1:T(8,128)(2,1)} copy(bf16[128,2,16384]{2,1,0:T(2,128)(2,1)} %reshape.125) | data formatting | bytes 16777216 | tf_op jit(solution)/shard_map/reshape | solution.py:43
  158.0 25.8 %fusion.21 = bf16[128,256,128]{2,1,0:T(8,128)(2,1)} fusion(bf16[128,128,2,128]{1,0,3,2:T(8,128)(2,1)} %bitcast.310, bf16[1,128,256]{1,2,0:T(8,128)(2,1)S(1)} %get-tuple-element.61, bf16[1,128,256]{1,2,0:T(8,128)(2,1)S(1)} %get-tuple-element.60), kind=kOutput, calls=%fused_computation.44 | convolution fusion | flops 2151940096 | bytes 16908288 | tf_op jit(solution)/shard_map/ijck,cjb->ibk/dot_general | solution.py:42
  183.8 12.9 %reshape.127 = bf16[128,2,16384]{2,1,0:T(2,128)(2,1)} reshape(bf16[128,256,128]{2,1,0:T(8,128)(2,1)} %fusion.21) | data formatting | bytes 16777216 | tf_op jit(solution)/shard_map/reshape | solution.py:43
  196.7 12.0 %copy.115 = bf16[128,2,16384]{2,0,1:T(8,128)(2,1)} copy(bf16[128,2,16384]{2,1,0:T(2,128)(2,1)} %reshape.127) | data formatting | bytes 16777216 | tf_op jit(solution)/shard_map/reshape | solution.py:43
  208.7 13.9 %pad_maximum_fusion = bf16[2,256,16384]{2,1,0:T(8,128)(2,1)} fusion(bf16[2,128,16384]{2,1,0:T(8,128)(2,1)} %bitcast.316, bf16[2,128,16384]{2,1,0:T(8,128)(2,1)} %bitcast.315), kind=kLoop, calls=%fused_computation.13 | loop fusion | flops 33554432 | bytes 33554432 | tf_op jit(solution)/shard_map/concatenate | solution.py:45
  222.5 40.8 %copy.59 = bf16[2,256,16384]{1,0,2:T(2,128)(2,1)} copy(bf16[2,256,16384]{2,1,0:T(8,128)(2,1)} %pad_maximum_fusion) | data formatting | bytes 33554432 | tf_op jit(solution)/shard_map/concatenate | solution.py:45
  290.7 25.8 %fusion.24 = bf16[128,256,128]{2,1,0:T(8,128)(2,1)} fusion(bf16[128,128,2,128]{1,0,3,2:T(8,128)(2,1)} %bitcast.313, bf16[1,128,256]{1,2,0:T(8,128)(2,1)S(1)} %get-tuple-element.65, bf16[1,128,256]{1,2,0:T(8,128)(2,1)S(1)} %get-tuple-element.64), kind=kOutput, calls=%fused_computation.45 | convolution fusion | flops 2151940096 | bytes 16908288 | tf_op jit(solution)/shard_map/ijck,cjb->ibk/dot_general | solution.py:42
  316.5 12.7 %reshape.129 = bf16[128,2,16384]{2,1,0:T(2,128)(2,1)} reshape(bf16[128,256,128]{2,1,0:T(8,128)(2,1)} %fusion.24) | data formatting | bytes 16777216 | tf_op jit(solution)/shard_map/reshape | solution.py:43
  329.2 12.0 %copy.114 = bf16[128,2,16384]{2,0,1:T(8,128)(2,1)} copy(bf16[128,2,16384]{2,1,0:T(2,128)(2,1)} %reshape.129) | data formatting | bytes 16777216 | tf_op jit(solution)/shard_map/reshape | solution.py:43
  359.4 25.8 %fusion.27 = bf16[128,256,128]{2,1,0:T(8,128)(2,1)} fusion(bf16[128,128,2,128]{1,0,3,2:T(8,128)(2,1)} %bitcast.311, bf16[1,128,256]{1,2,0:T(8,128)(2,1)S(1)} %get-tuple-element.69, bf16[1,128,256]{1,2,0:T(8,128)(2,1)S(1)} %get-tuple-element.68), kind=kOutput, calls=%fused_computation.46 | convolution fusion | flops 2151940096 | bytes 16908288 | tf_op jit(solution)/shard_map/ijck,cjb->ibk/dot_general | solution.py:42
  385.2 13.0 %reshape.131 = bf16[128,2,16384]{2,1,0:T(2,128)(2,1)} reshape(bf16[128,256,128]{2,1,0:T(8,128)(2,1)} %fusion.27) | data formatting | bytes 16777216 | tf_op jit(solution)/shard_map/reshape | solution.py:43
  398.2 12.0 %copy.113 = bf16[128,2,16384]{2,0,1:T(8,128)(2,1)} copy(bf16[128,2,16384]{2,1,0:T(2,128)(2,1)} %reshape.131) | data formatting | bytes 16777216 | tf_op jit(solution)/shard_map/reshape | solution.py:43
  410.1 13.8 %pad_maximum_fusion.1 = bf16[2,256,16384]{2,1,0:T(8,128)(2,1)} fusion(bf16[2,128,16384]{2,1,0:T(8,128)(2,1)} %bitcast.317, bf16[2,128,16384]{2,1,0:T(8,128)(2,1)} %bitcast.314), kind=kLoop, calls=%fused_computation.14 | loop fusion | flops 33554432 | bytes 33554432 | tf_op jit(solution)/shard_map/concatenate | solution.py:45
  424.0 40.7 %copy.69 = bf16[2,256,16384]{1,0,2:T(2,128)(2,1)} copy(bf16[2,256,16384]{2,1,0:T(8,128)(2,1)} %pad_maximum_fusion.1) | data formatting | bytes 33554432 | tf_op jit(solution)/shard_map/concatenate | solution.py:45
  464.7 168.9 %all-to-all-done = bf16[2,1,256,16384]{2,0,1,3:T(2,128)(2,1)} async-done(((bf16[2,1,256,16384]{2,0,1,3:T(2,128)(2,1)}), bf16[2,1,256,16384]{2,0,1,3:T(2,128)(2,1)}, u32[]{:S(2)}, u32[]{:S(2)}) %all-to-all-start) | async-done | bytes 16777248 | tf_op jit(solution)/shard_map/all_to_all | solution.py:51
  639.7 23.5 %fusion.83 = (bf16[2,1,2048,2048]{3,2,1,0:T(8,128)(2,1)}, bf16[2,1,2048,2048]{3,2,1,0:T(8,128)(2,1)}) fusion(bf16[2,2,2048,2048]{3,2,1,0:T(8,128)(2,1)} %param.8), kind=kLoop, calls=%fused_computation.163 | loop fusion | bytes 67108864 | tf_op jit(solution)/shard_map/slice | solution.py:55
  663.2 13.1 %gather_fusion.3 = bf16[16,2,128,2048]{3,2,1,0:T(8,128)(2,1)} fusion(bf16[2,16,128,2048]{3,2,1,0:T(8,128)(2,1)} %bitcast.309, s32[1024]{0:T(1024)S(1)} %pad_clamp_fusion), kind=kCustom, calls=%fused_computation.clone | custom fusion | bytes 33554496 | tf_op jit(solution)/shard_map/jit(_take)/gather | solution.py:56
  676.4 13.1 %gather_fusion.4 = bf16[16,2,128,2048]{3,2,1,0:T(8,128)(2,1)} fusion(bf16[2,16,128,2048]{3,2,1,0:T(8,128)(2,1)} %bitcast.308, s32[1024]{0:T(1024)S(1)} %pad_clamp_fusion), kind=kCustom, calls=%fused_computation.1.clone | custom fusion | bytes 33554496 | tf_op jit(solution)/shard_map/jit(_take)/gather | solution.py:56
  690.2 23.2 %fusion.5 = (bf16[2,16,128,2048]{3,2,1,0:T(8,128)(2,1)}, bf16[2,16,128,2048]{3,2,1,0:T(8,128)(2,1)}) fusion(bf16[16,2,128,2048]{3,2,1,0:T(8,128)(2,1)} %gather_fusion.3, pred[16]{0:T(512)(128)(4,1)S(1)} %compare_and_fusion, bf16[16,2,128,2048]{3,2,1,0:T(8,128)(2,1)} %gather_fusion.4), kind=kLoop, calls=%fused_computation.22 | loop fusion | flops 16777216 | bytes 67108880 | tf_op jit(solution)/shard_map/jit(_take)/select_n | solution.py:56
  722.0 41.0 %copy.60 = bf16[2,1,256,8,2048]{4,2,3,1,0:T(8,128)(2,1)} copy(bf16[2,1,256,8,2048]{2,0,4,3,1:T(2,128)(2,1)} %bitcast.46) | data formatting | bytes 33554432 | tf_op jit(solution)/shard_map/all_to_all | solution.py:51
  763.0 9.4 fusion.84
  772.4 12.2 %fusion.10 = f32[16,128,128]{2,1,0:T(8,128)} fusion(bf16[16,128,2048]{2,1,0:T(8,128)(2,1)} %bitcast.324, bf16[2,16,128,2048]{3,2,1,0:T(8,128)(2,1)} %get-tuple-element.84), kind=kOutput, calls=%fused_computation.35 | convolution fusion | flops 1073741824 | bytes 17825792 | tf_op jit(solution)/shard_map/oic,ojc->oij/dot_general | solution.py:60
  798.5 204.9 %all-to-all-done.1 = bf16[2,1,256,16384]{2,0,1,3:T(2,128)(2,1)} async-done(((bf16[2,1,256,16384]{2,0,1,3:T(2,128)(2,1)}), bf16[2,1,256,16384]{2,0,1,3:T(2,128)(2,1)}, u32[]{:S(2)}, u32[]{:S(2)}) %all-to-all-start.1) | async-done | bytes 16777248 | tf_op jit(solution)/shard_map/all_to_all | solution.py:51
  1003.3 41.0 %copy.70 = bf16[2,1,256,8,2048]{4,2,3,1,0:T(8,128)(2,1)} copy(bf16[2,1,256,8,2048]{2,0,4,3,1:T(2,128)(2,1)} %bitcast.92) | data formatting | bytes 33554432 | tf_op jit(solution)/shard_map/all_to_all | solution.py:51
  1044.3 9.6 fusion.85
  1053.9 12.1 %fusion.14 = f32[16,128,128]{2,1,0:T(8,128)} fusion(bf16[16,128,2048]{2,1,0:T(8,128)(2,1)} %bitcast.322, bf16[2,16,128,2048]{3,2,1,0:T(8,128)(2,1)} %get-tuple-element.85), kind=kOutput, calls=%fused_computation.39 | convolution fusion | flops 1073741824 | bytes 17825792 | tf_op jit(solution)/shard_map/oic,ojc->oij/dot_general | solution.py:60
  1099.2 14.5 %psum.7 = f32[2,1,2,16,1]{3,2,0,4,1:T(2,128)S(1)} all-reduce(f32[2,1,2,16,1]{3,2,0,4,1:T(2,128)S(1)} %bitcast.328), channel_id=1, replica_groups=mesh['tm'=4,'op'=8] {'op'}, use_global_device_ids=true, to_apply=%region_4.6 | all-reduce | flops 64 | bytes 512 | tf_op jit(solution)/shard_map/psum | solution.py:76
  (74 shorter events, 161.8 us)
Async XLA Ops:
  6.5 52.9 %all-gather.2.cloned.1.call-start = ((), (), s32[]{:S(2)}) async-start(), calls=%async_computation.2 | async-start | bytes 2359296 | tf_op jit(solution)/shard_map/all_gather | solution.py:20
  70.5 9.4 copy-start.3
  263.4 370.3 %all-to-all-start = ((bf16[2,1,256,16384]{2,0,1,3:T(2,128)(2,1)}), bf16[2,1,256,16384]{2,0,1,3:T(2,128)(2,1)}, u32[]{:S(2)}, u32[]{:S(2)}) async-start(bf16[2,1,256,16384]{2,0,1,3:T(2,128)(2,1)} %bitcast.304), calls=%async_computation | async-start | bytes 33554432 | tf_op jit(solution)/shard_map/all_to_all | solution.py:51
  633.6 6.1 copy-start.7
  633.7 369.7 %all-to-all-start.1 = ((bf16[2,1,256,16384]{2,0,1,3:T(2,128)(2,1)}), bf16[2,1,256,16384]{2,0,1,3:T(2,128)(2,1)}, u32[]{:S(2)}, u32[]{:S(2)}) async-start(bf16[2,1,256,16384]{2,0,1,3:T(2,128)(2,1)} %bitcast.305), calls=%async_computation.1 | async-start | bytes 33554432 | tf_op jit(solution)/shard_map/all_to_all | solution.py:51
  676.4 13.1 %copy-start = (s32[16,3]{0,1:T(4,128)S(1)}, s32[16,3]{0,1:T(4,128)}, u32[]{:S(2)}) copy-start(s32[16,3]{0,1:T(4,128)} %param.11) | copy-start | bytes 580
  690.1 23.2 %copy-start.4 = (bf16[2,1,1,512,512]{3,4,2,1,0:T(8,128)(2,1)S(1)}, bf16[2,1,1,512,512]{3,4,2,1,0:T(8,128)(2,1)}, u32[]{:S(2)}) copy-start(bf16[2,1,1,512,512]{3,4,2,1,0:T(8,128)(2,1)} %copy-done.3) | copy-start | bytes 3145732
  772.4 12.2 %copy-start.1 = (bf16[1,1,8,256,2048]{4,3,2,1,0:T(8,128)(2,1)}, bf16[1,1,8,256,2048]{4,3,2,1,0:T(8,128)(2,1)S(1)}, u32[]{:S(2)}) copy-start(bf16[1,1,8,256,2048]{4,3,2,1,0:T(8,128)(2,1)S(1)} %get-tuple-element.28) | copy-start | bytes 25165828
  1053.9 12.1 %copy-start.2 = (bf16[1,1,8,256,2048]{4,3,2,1,0:T(8,128)(2,1)}, bf16[1,1,8,256,2048]{4,3,2,1,0:T(8,128)(2,1)S(1)}, u32[]{:S(2)}) copy-start(bf16[1,1,8,256,2048]{4,3,2,1,0:T(8,128)(2,1)S(1)} %get-tuple-element.30) | copy-start | bytes 25165828
  1072.8 8.5 copy-start.6
  1081.3 9.0 copy-start.5
Sparse Core Ops, SparseCore 0:
  8.9 31.8 all-gather.1
where the time goes:
time: 1130 us; the launch traced here: 1120 us
  local copies, waits for them, and re-layouts  432 us (38%)
  waiting for transfers between devices  374 us (33%)
  matrix products  211 us (19%)
  other arithmetic  54.8 us (5%)
  between operations  22.9 us (2%)
  blocking collectives  14.5 us (1%)
  starting transfers between devices  12.5 us (1%)
    all_to_all x2, waiting for transfers between devices, on_device(): lax.all_to_all(stacked, 'op', split_axis=3, concat_axis=2, tiled=True)  374 us
    dot_general x4, matrix products, sink_side(): jnp.einsum('ijck,cjb->ibk', x_both, second, preferred_element_type=jnp.fl...  103 us
    reshape x8, local copies, waits for them, and re-layouts, sink_side(): y_both = y_both.astype(jnp.bfloat16).reshape(span, 2, NEV * NEV)  99.1 us
    all_to_all x2, local copies, waits for them, and re-layouts, on_device(): lax.all_to_all(stacked, 'op', split_axis=3, concat_axis=2, tiled=True)  82 us
    concatenate x2, local copies, waits for them, and re-layouts, sink_side(): return jnp.concatenate(pieces, axis=1)  81.6 us
    dot_general x8, matrix products, inner(): return jnp.einsum('oic,ojc->oij', a, b, preferred_element_type=jnp.float32)  71.2 us
    unnamed x23, local copies, waits for them, and re-layouts  45.9 us
    dot_general x4, matrix products, sink_side(): jnp.einsum('cxk,ckb->xb', phi, third, preferred_element_type=jnp.float32)  36.2 us
  transfers between devices with their start and end apart: 3, of which 2 were waited for; matrix products, arithmetic and copies ran while one was open for 35% of the time, Pallas kernels for 0%

commit v1 on v0

--- a/solution.py
+++ b/solution.py
@@ -48,7 +48,9 @@
     for t0 in range(TSRC):
         combos = [(local, t0, p) for local in range(local_times) for p in range(PAIRS)]
         stacked = jnp.stack([sink_side(local, t0, p) for local, t0, p in combos], axis=1)
-        columns = lax.all_to_all(stacked, "op", split_axis=3, concat_axis=2, tiled=True)
+        parts = jnp.split(stacked, lax.axis_size("op"), axis=3)
+        incoming = lax.all_to_all(jnp.stack(parts), "op", 0, 0)
+        columns = jnp.concatenate(incoming, axis=2)
         for index, combo in enumerate(combos):
             column_t0 = combo[1]
             other = pair_list[:, combo[2]]

time: 1130 us -> 1060 us (0.938)
  local copies, waits for them, and re-layouts: 432 us -> 300 us
  waiting for transfers between devices: 374 us -> 445 us
    concatenate x2 -> x0, local copies, waits for them, and re-layouts: 81.6 us -> none  [sink_side(): return jnp.concatenate(pieces, axis=1)]
    all_to_all x2, waiting for transfers between devices: 374 us -> 445 us  [on_device(): incoming = lax.all_to_all(jnp.stack(parts), 'op', 0, 0)]
    all_to_all x2, local copies, waits for them, and re-layouts: 82 us -> 16.8 us  [on_device(): incoming = lax.all_to_all(jnp.stack(parts), 'op', 0, 0)]
    concatenate x2 -> x0, other arithmetic: 27.7 us -> none  [sink_side(): return jnp.concatenate(pieces, axis=1)]
    unnamed x23 -> x37, local copies, waits for them, and re-layouts: 45.9 us -> 68.1 us
    another operation x0 -> x2, other arithmetic: none -> 16.6 us  [on_device(): jnp.stack([sink_side(local, t0, p) for local, t0, p in combos], axis=1)]
  transfers between devices with their start and end apart: 3 -> 3, of which waited for: 2 -> 2; matrix products, arithmetic and copies ran while one was open for 35% -> 31% of each run, Pallas kernels for 0% -> 0%
where the time goes in v1:
time: 1060 us; the launch traced here: 1050 us
  waiting for transfers between devices  445 us (42%)
  local copies, waits for them, and re-layouts  300 us (28%)
  matrix products  211 us (20%)
  other arithmetic  43.7 us (4%)
  between operations  23.1 us (2%)
  blocking collectives  14.5 us (1%)
  starting transfers between devices  12.3 us (1%)
    all_to_all x2, waiting for transfers between devices, on_device(): incoming = lax.all_to_all(jnp.stack(parts), 'op', 0, 0)  445 us
    dot_general x4, matrix products, sink_side(): jnp.einsum('ijck,cjb->ibk', x_both, second, preferred_element_type=jnp.fl...  104 us
    reshape x8, local copies, waits for them, and re-layouts, sink_side(): y_both = y_both.astype(jnp.bfloat16).reshape(span, 2, NEV * NEV)  98.8 us
    dot_general x8, matrix products, inner(): return jnp.einsum('oic,ojc->oij', a, b, preferred_element_type=jnp.float32)  71.1 us
    unnamed x37, local copies, waits for them, and re-layouts  68.1 us
    dot_general x4, matrix products, sink_side(): jnp.einsum('cxk,ckb->xb', phi, third, preferred_element_type=jnp.float32)  36.3 us
    another operation x2, local copies, waits for them, and re-layouts, sink_side(): sink_elem[:, local, group * span:(group + 1) * span]  26.9 us
    gather x2, local copies, waits for them, and re-layouts, on_device(): chosen = jnp.take(source, other, axis=1)  26.2 us
  transfers between devices with their start and end apart: 3, of which 2 were waited for; matrix products, arithmetic and copies ran while one was open for 31% of the time, Pallas kernels for 0%

profile of v1, /device:TPU:0, one launch (start us, length us, event | category | flops | bytes accessed | tf_op | source)
XLA Modules:
  0.0 1050.1 jit_solution(15477032726458004033)
XLA Ops:
  20.9 11.6 %fusion.102 = (bf16[2,1,128,16384]{3,2,1,0:T(8,128)(2,1)}, bf16[2,1,128,16384]{3,2,1,0:T(8,128)(2,1)}) fusion(bf16[2,1,256,16384]{3,2,1,0:T(8,128)(2,1)} %param.7), kind=kLoop, calls=%fused_computation.200 | loop fusion | bytes 33554432 | tf_op jit(solution)/shard_map/slice | solution.py:39
  32.5 13.5 %reshape_squeeze.21 = bf16[2,16384,128]{2,1,0:T(8,128)(2,1)} reshape(bf16[2,1,128,16384]{3,2,1,0:T(8,128)(2,1)} %get-tuple-element.32) | data formatting | bytes 16777216 | tf_op jit(solution)/shard_map/reshape;squeeze | solution.py:39
  45.9 13.5 %reshape_squeeze.22 = bf16[2,16384,128]{2,1,0:T(8,128)(2,1)} reshape(bf16[2,1,128,16384]{3,2,1,0:T(8,128)(2,1)} %get-tuple-element.33) | data formatting | bytes 16777216 | tf_op jit(solution)/shard_map/reshape;squeeze | solution.py:39
  70.7 9.2 fusion.33
  79.9 9.2 copy.85
  89.1 26.0 %fusion.18 = bf16[128,256,128]{2,1,0:T(8,128)(2,1)} fusion(bf16[128,128,2,128]{1,0,3,2:T(8,128)(2,1)} %bitcast.406, bf16[1,128,256]{1,2,0:T(8,128)(2,1)S(1)} %get-tuple-element.57, bf16[1,128,256]{1,2,0:T(8,128)(2,1)S(1)} %get-tuple-element.56), kind=kOutput, calls=%fused_computation.45 | convolution fusion | flops 2151940096 | bytes 16908288 | tf_op jit(solution)/shard_map/ijck,cjb->ibk/dot_general | solution.py:42
  115.1 12.7 %reshape.129 = bf16[128,2,16384]{2,1,0:T(2,128)(2,1)} reshape(bf16[128,256,128]{2,1,0:T(8,128)(2,1)} %fusion.18) | data formatting | bytes 16777216 | tf_op jit(solution)/shard_map/reshape | solution.py:43
  127.8 12.0 %copy.125 = bf16[128,2,16384]{2,0,1:T(8,128)(2,1)} copy(bf16[128,2,16384]{2,1,0:T(2,128)(2,1)} %reshape.129) | data formatting | bytes 16777216 | tf_op jit(solution)/shard_map/reshape | solution.py:43
  139.8 9.0 fusion.32
  148.8 9.2 copy.86
  158.0 25.8 %fusion.21 = bf16[128,256,128]{2,1,0:T(8,128)(2,1)} fusion(bf16[128,128,2,128]{1,0,3,2:T(8,128)(2,1)} %bitcast.404, bf16[1,128,256]{1,2,0:T(8,128)(2,1)S(1)} %get-tuple-element.61, bf16[1,128,256]{1,2,0:T(8,128)(2,1)S(1)} %get-tuple-element.60), kind=kOutput, calls=%fused_computation.46 | convolution fusion | flops 2151940096 | bytes 16908288 | tf_op jit(solution)/shard_map/ijck,cjb->ibk/dot_general | solution.py:42
  183.8 12.9 %reshape.131 = bf16[128,2,16384]{2,1,0:T(2,128)(2,1)} reshape(bf16[128,256,128]{2,1,0:T(8,128)(2,1)} %fusion.21) | data formatting | bytes 16777216 | tf_op jit(solution)/shard_map/reshape | solution.py:43
  196.7 12.0 %copy.124 = bf16[128,2,16384]{2,0,1:T(8,128)(2,1)} copy(bf16[128,2,16384]{2,1,0:T(2,128)(2,1)} %reshape.131) | data formatting | bytes 16777216 | tf_op jit(solution)/shard_map/reshape | solution.py:43
  238.8 9.0 fusion.31
  247.8 9.2 copy.87
  257.0 25.8 %fusion.24 = bf16[128,256,128]{2,1,0:T(8,128)(2,1)} fusion(bf16[128,128,2,128]{1,0,3,2:T(8,128)(2,1)} %bitcast.407, bf16[1,128,256]{1,2,0:T(8,128)(2,1)S(1)} %get-tuple-element.65, bf16[1,128,256]{1,2,0:T(8,128)(2,1)S(1)} %get-tuple-element.64), kind=kOutput, calls=%fused_computation.47 | convolution fusion | flops 2151940096 | bytes 16908288 | tf_op jit(solution)/shard_map/ijck,cjb->ibk/dot_general | solution.py:42
  282.8 12.7 %reshape.134 = bf16[128,2,16384]{2,1,0:T(2,128)(2,1)} reshape(bf16[128,256,128]{2,1,0:T(8,128)(2,1)} %fusion.24) | data formatting | bytes 16777216 | tf_op jit(solution)/shard_map/reshape | solution.py:43
  295.5 11.9 %copy.123 = bf16[128,2,16384]{2,0,1:T(8,128)(2,1)} copy(bf16[128,2,16384]{2,1,0:T(2,128)(2,1)} %reshape.134) | data formatting | bytes 16777216 | tf_op jit(solution)/shard_map/reshape | solution.py:43
  307.4 9.0 fusion.30
  316.4 9.2 copy.88
  325.7 26.0 %fusion.27 = bf16[128,256,128]{2,1,0:T(8,128)(2,1)} fusion(bf16[128,128,2,128]{1,0,3,2:T(8,128)(2,1)} %bitcast.405, bf16[1,128,256]{1,2,0:T(8,128)(2,1)S(1)} %get-tuple-element.69, bf16[1,128,256]{1,2,0:T(8,128)(2,1)S(1)} %get-tuple-element.68), kind=kOutput, calls=%fused_computation.48 | convolution fusion | flops 2151940096 | bytes 16908288 | tf_op jit(solution)/shard_map/ijck,cjb->ibk/dot_general | solution.py:42
  351.7 12.7 %reshape.136 = bf16[128,2,16384]{2,1,0:T(2,128)(2,1)} reshape(bf16[128,256,128]{2,1,0:T(8,128)(2,1)} %fusion.27) | data formatting | bytes 16777216 | tf_op jit(solution)/shard_map/reshape | solution.py:43
  364.3 12.0 %copy.122 = bf16[128,2,16384]{2,0,1:T(8,128)(2,1)} copy(bf16[128,2,16384]{2,1,0:T(2,128)(2,1)} %reshape.136) | data formatting | bytes 16777216 | tf_op jit(solution)/shard_map/reshape | solution.py:43
  397.3 202.7 %all-to-all-done = bf16[8,2,1,256,2048]{4,3,2,1,0:T(8,128)(2,1)} async-done(((bf16[8,2,1,256,2048]{4,3,2,1,0:T(8,128)(2,1)}), bf16[8,2,1,256,2048]{4,3,2,1,0:T(8,128)(2,1)}, u32[]{:S(2)}, u32[]{:S(2)}) %all-to-all-start) | async-done | bytes 16777248 | tf_op jit(solution)/shard_map/all_to_all | solution.py:52
  605.9 23.5 %fusion.99 = (bf16[2,1,2048,2048]{3,2,1,0:T(8,128)(2,1)}, bf16[2,1,2048,2048]{3,2,1,0:T(8,128)(2,1)}) fusion(bf16[2,2,2048,2048]{3,2,1,0:T(8,128)(2,1)} %param.8), kind=kLoop, calls=%fused_computation.197 | loop fusion | bytes 67108864 | tf_op jit(solution)/shard_map/slice | solution.py:57
  629.4 13.1 %gather_fusion.3 = bf16[16,2,128,2048]{3,2,1,0:T(8,128)(2,1)} fusion(bf16[2,16,128,2048]{3,2,1,0:T(8,128)(2,1)} %bitcast.403, s32[1024]{0:T(1024)S(1)} %pad_clamp_fusion), kind=kCustom, calls=%fused_computation.clone | custom fusion | bytes 33554496 | tf_op jit(solution)/shard_map/jit(_take)/gather | solution.py:58
  642.5 13.1 %gather_fusion.4 = bf16[16,2,128,2048]{3,2,1,0:T(8,128)(2,1)} fusion(bf16[2,16,128,2048]{3,2,1,0:T(8,128)(2,1)} %bitcast.402, s32[1024]{0:T(1024)S(1)} %pad_clamp_fusion), kind=kCustom, calls=%fused_computation.1.clone | custom fusion | bytes 33554496 | tf_op jit(solution)/shard_map/jit(_take)/gather | solution.py:58
  656.4 23.2 %fusion.5 = (bf16[2,16,128,2048]{3,2,1,0:T(8,128)(2,1)}, bf16[2,16,128,2048]{3,2,1,0:T(8,128)(2,1)}) fusion(bf16[16,2,128,2048]{3,2,1,0:T(8,128)(2,1)} %gather_fusion.3, pred[16]{0:T(512)(128)(4,1)S(1)} %compare_and_fusion, bf16[16,2,128,2048]{3,2,1,0:T(8,128)(2,1)} %gather_fusion.4), kind=kLoop, calls=%fused_computation.23 | loop fusion | flops 16777216 | bytes 67108880 | tf_op jit(solution)/shard_map/jit(_take)/select_n | solution.py:58
  700.9 12.1 %fusion.10 = f32[16,128,128]{2,1,0:T(8,128)} fusion(bf16[16,128,2048]{2,1,0:T(8,128)(2,1)} %bitcast.418, bf16[2,16,128,2048]{3,2,1,0:T(8,128)(2,1)} %get-tuple-element.84), kind=kOutput, calls=%fused_computation.37 | convolution fusion | flops 1073741824 | bytes 17825792 | tf_op jit(solution)/shard_map/oic,ojc->oij/dot_general | solution.py:62
  726.9 242.6 %all-to-all-done.1 = bf16[8,2,1,256,2048]{4,3,2,1,0:T(8,128)(2,1)} async-done(((bf16[8,2,1,256,2048]{4,3,2,1,0:T(8,128)(2,1)}), bf16[8,2,1,256,2048]{4,3,2,1,0:T(8,128)(2,1)}, u32[]{:S(2)}, u32[]{:S(2)}) %all-to-all-start.1) | async-done | bytes 16777248 | tf_op jit(solution)/shard_map/all_to_all | solution.py:52
  982.5 12.1 %fusion.14 = f32[16,128,128]{2,1,0:T(8,128)} fusion(bf16[16,128,2048]{2,1,0:T(8,128)(2,1)} %bitcast.416, bf16[2,16,128,2048]{3,2,1,0:T(8,128)(2,1)} %get-tuple-element.85), kind=kOutput, calls=%fused_computation.41 | convolution fusion | flops 1073741824 | bytes 17825792 | tf_op jit(solution)/shard_map/oic,ojc->oij/dot_general | solution.py:62
  1027.8 14.5 %psum.7 = f32[2,1,2,16,1]{3,2,0,4,1:T(2,128)S(1)} all-reduce(f32[2,1,2,16,1]{3,2,0,4,1:T(2,128)S(1)} %bitcast.422), channel_id=1, replica_groups=mesh['tm'=4,'op'=8] {'op'}, use_global_device_ids=true, to_apply=%region_4.6 | all-reduce | flops 64 | bytes 512 | tf_op jit(solution)/shard_map/psum | solution.py:78
  (88 shorter events, 156.2 us)
Async XLA Ops:
  6.5 52.9 %all-gather.2.cloned.1.call-start = ((), (), s32[]{:S(2)}) async-start(), calls=%async_computation.2 | async-start | bytes 2359296 | tf_op jit(solution)/shard_map/all_gather | solution.py:20
  70.5 9.4 copy-start.3
  229.7 370.3 %all-to-all-start = ((bf16[8,2,1,256,2048]{4,3,2,1,0:T(8,128)(2,1)}), bf16[8,2,1,256,2048]{4,3,2,1,0:T(8,128)(2,1)}, u32[]{:S(2)}, u32[]{:S(2)}) async-start(bf16[8,2,1,256,2048]{4,3,2,1,0:T(8,128)(2,1)} %fusion.42), calls=%async_computation | async-start | bytes 33554432 | tf_op jit(solution)/shard_map/all_to_all | solution.py:52
  397.3 208.6 %copy-start.7 = (s32[16,1]{0,1:T(1,128)S(1)}, s32[16,1]{0,1:T(1,128)}, u32[]{:S(2)}) copy-start(s32[16,1]{0,1:T(1,128)} %param.10) | copy-start | bytes 196
  600.0 369.6 %all-to-all-start.1 = ((bf16[8,2,1,256,2048]{4,3,2,1,0:T(8,128)(2,1)}), bf16[8,2,1,256,2048]{4,3,2,1,0:T(8,128)(2,1)}, u32[]{:S(2)}, u32[]{:S(2)}) async-start(bf16[8,2,1,256,2048]{4,3,2,1,0:T(8,128)(2,1)} %fusion.34), calls=%async_computation.1 | async-start | bytes 33554432 | tf_op jit(solution)/shard_map/all_to_all | solution.py:52
  642.5 13.1 %copy-start = (s32[16,3]{0,1:T(4,128)S(1)}, s32[16,3]{0,1:T(4,128)}, u32[]{:S(2)}) copy-start(s32[16,3]{0,1:T(4,128)} %param.11) | copy-start | bytes 580
  656.4 23.2 %copy-start.4 = (bf16[2,1,1,512,512]{3,4,2,1,0:T(8,128)(2,1)S(1)}, bf16[2,1,1,512,512]{3,4,2,1,0:T(8,128)(2,1)}, u32[]{:S(2)}) copy-start(bf16[2,1,1,512,512]{3,4,2,1,0:T(8,128)(2,1)} %copy-done.3) | copy-start | bytes 3145732
  700.9 12.1 %copy-start.1 = (bf16[1,1,8,256,2048]{4,3,2,1,0:T(8,128)(2,1)}, bf16[1,1,8,256,2048]{4,3,2,1,0:T(8,128)(2,1)S(1)}, u32[]{:S(2)}) copy-start(bf16[1,1,8,256,2048]{4,3,2,1,0:T(8,128)(2,1)S(1)} %get-tuple-element.28) | copy-start | bytes 25165828
  982.5 12.1 %copy-start.2 = (bf16[1,1,8,256,2048]{4,3,2,1,0:T(8,128)(2,1)}, bf16[1,1,8,256,2048]{4,3,2,1,0:T(8,128)(2,1)S(1)}, u32[]{:S(2)}) copy-start(bf16[1,1,8,256,2048]{4,3,2,1,0:T(8,128)(2,1)S(1)} %get-tuple-element.30) | copy-start | bytes 25165828
  1001.3 8.5 copy-start.6
  1009.8 9.0 copy-start.5
Sparse Core Ops, SparseCore 0:
  8.9 31.8 all-gather.1
